TPU v7x, 32 devices: a whole 2x2x4 slice. The times are simulated.
32 devices in a mesh: expert: 4 (over z), tensor: 4 (over y, x), dp: 2 (over core).
Axes of the slice: x: 2, y: 2, z: 4, core: 2. Of those that a mesh axis runs over, the one named last changes fastest.
Arguments:
- tokens: bfloat16 [4096, 2048], P(('dp', 'expert', 'tensor')), parts along dimension 0, may hold values from -6 to 6
- expert_ids: int32 [4096, 4], P(('dp', 'expert', 'tensor')), parts along dimension 0, may hold values from 0 to 15, all different within a row; in each aligned block of 128 rows (0 to 127, 128 to 255, ...) at most 64 rows name the same one
- gate_probs: float32 [4096, 4], P(('dp', 'expert', 'tensor')), parts along dimension 0, may hold values from 0.05 to 0.6
- w_gate: bfloat16 [16, 2048, 1408], P(('expert', 'tensor')), may hold values from -0.125 to 0.125
- w_up: bfloat16 [16, 2048, 1408], P(('expert', 'tensor')), may hold values from -0.125 to 0.125
- w_down: bfloat16 [16, 1408, 2048], P(('expert', 'tensor')), may hold values from -0.15625 to 0.15625
- s_gate: bfloat16 [2048, 2816], P(None, 'tensor'), may hold values from -0.125 to 0.125
- s_up: bfloat16 [2048, 2816], P(None, 'tensor'), may hold values from -0.125 to 0.125
- s_down: bfloat16 [2816, 2048], P('tensor'), may hold values from -0.109375 to 0.109375
- shared_gate: bfloat16 [2048], replicated, may hold values from -0.125 to 0.125
Outputs:
- mixed: bfloat16 [4096, 2048], P(('dp', 'expert', 'tensor')), parts along dimension 0
There are 2 independent parts, one for each index of `dp`. A program takes and returns all parts, laid end to end along the dimension named above; an argument that names none is the same for every part. Nothing has to cross between parts.
Inputs may be any that keep to these rules, and one draw needn't show every extreme that they name: `expert_ids`: among the rows of one device, no expert is named by more than 64 of them.
All inputs are finite; a program needn't handle non-finite values.
Results may differ from a plain program's by a relative error of at most 0.0095.
Values may be sent and summed in bfloat16 or wider, within the bound.
A program may use at most 128 MiB of HBM per device.

v0:
```python
import jax
import jax.numpy as jnp
from jax import lax
from jax.sharding import PartitionSpec as P


def silu_product(rows, w_first, w_second):
    gate = jnp.dot(rows, w_first, preferred_element_type=jnp.float32)
    up = jnp.dot(rows, w_second, preferred_element_type=jnp.float32)
    return (jax.nn.silu(gate) * up).astype(jnp.bfloat16)


def slot_index(ids, experts, capacity):
    flat = ids.reshape(-1)
    onehot = (flat[:, None] == jnp.arange(experts, dtype=jnp.int32)[None, :]).astype(jnp.int32)
    before = jnp.cumsum(onehot, axis=0) - onehot
    return flat * capacity + jnp.sum(before * onehot, axis=1)


def per_device(
    tokens, expert_ids, gate_probs, w_gate, w_up, w_down, s_gate, s_up, s_down, shared_gate
):
    tok_dev, width = tokens.shape
    top = expert_ids.shape[1]
    n_expert = lax.axis_size("expert")
    n_tensor = lax.axis_size("tensor")
    experts = n_expert * n_tensor
    capacity = max(2, 2 * top * tok_dev // experts)
    own_gate = w_gate[0]
    own_up = w_up[0]
    own_down = w_down[0]
    slot = slot_index(expert_ids, experts, capacity)
    repeated = jnp.repeat(tokens, top, axis=0)
    outgoing = jnp.zeros((experts * capacity, width), jnp.bfloat16).at[slot].set(repeated)
    outgoing = outgoing.reshape(experts, capacity, width)
    received = lax.all_to_all(
        outgoing, ("expert", "tensor"), split_axis=0, concat_axis=0, tiled=True
    )
    shape = received.shape
    flat_rows = received.reshape(-1, width)
    hidden = silu_product(flat_rows, own_gate, own_up)
    done = jnp.dot(hidden, own_down, preferred_element_type=jnp.float32).astype(jnp.bfloat16)
    finished = done.reshape(shape)
    back = lax.all_to_all(finished, ("expert", "tensor"), split_axis=0, concat_axis=0, tiled=True)
    picked = back.reshape(experts * capacity, width)[slot].reshape(tok_dev, top, width)
    routed = jnp.einsum("tk,tkd->td", gate_probs, picked.astype(jnp.float32))
    shared_hidden = silu_product(lax.all_gather(tokens, "tensor", axis=0, tiled=True), s_gate, s_up)
    shared = lax.psum_scatter(
        jnp.dot(shared_hidden, s_down, preferred_element_type=jnp.float32).astype(jnp.bfloat16),
        "tensor",
        scatter_dimension=0,
        tiled=True,
    ).astype(jnp.float32)
    scale = jax.nn.sigmoid(jnp.dot(tokens, shared_gate, preferred_element_type=jnp.float32))
    return (scale[:, None] * shared + routed).astype(jnp.bfloat16)


def solution(mesh):
    return jax.shard_map(
        per_device,
        mesh=mesh,
        in_specs=(
            P(("dp", "expert", "tensor"), None),
            P(("dp", "expert", "tensor"), None),
            P(("dp", "expert", "tensor"), None),
            P(("expert", "tensor"), None, None),
            P(("expert", "tensor"), None, None),
            P(("expert", "tensor"), None, None),
            P(None, "tensor"),
            P(None, "tensor"),
            P("tensor", None),
            P(),
        ),
        out_specs=P(("dp", "expert", "tensor"), None),
        check_vma=False,
    )
```

profile of v0, /device:TPU:14, one launch (start us, length us, event | category | flops | bytes accessed | tf_op | source)
XLA Modules:
  0.0 281.9 jit_solution(9944033376848571911)
XLA Ops:
  6.5 0.0 copy-start
  6.5 0.9 copy.12
  7.5 0.1 eq.29
  7.6 0.1 eq.25
  7.7 0.7 broadcast_multiply_fusion
  8.4 1.1 reduce-window.6
  9.5 0.2 slice_reduce_fusion
  9.8 0.1 copy.11
  9.9 0.1 mul.47
  10.0 3.4 %broadcast_in_dim.5 = bf16[128,4,2048]{2,1,0:T(4,128)(2,1)} broadcast(bf16[128,2048]{1,0:T(8,128)(2,1)} %param.10), dimensions={0,2} | broadcast | bytes 2621440 | tf_op jit(solution)/shard_map/broadcast_in_dim | solution.py:33
  13.5 4.0 %reshape.84 = bf16[512,2048]{1,0:T(8,128)(2,1)} reshape(bf16[128,4,2048]{2,1,0:T(4,128)(2,1)} %broadcast_in_dim.5) | data formatting | bytes 4194304 | tf_op jit(solution)/shard_map/reshape | solution.py:33
  17.4 0.1 fusion.26
  17.5 7.2 %scatter_custom_fusion = bf16[1024,2048]{1,0:T(8,128)(2,1)} fusion(s32[512]{0:T(512)S(1)} %bitcast.70, bf16[512,2048]{1,0:T(8,128)(2,1)} %reshape.84, bf16[]{:T(256)} %constant.6.clone.1), kind=kCustom, calls=%fused_computation.12 | custom fusion | bytes 4194816 | tf_op jit(solution)/shard_map/scatter | solution.py:34
  24.7 7.1 %all-to-all-start = ((bf16[16,64,2048]{2,1,0:T(8,128)(2,1)}), bf16[16,64,2048]{2,1,0:T(8,128)(2,1)}, u32[]{:S(2)}, u32[]{:S(2)}) async-start(bf16[16,64,2048]{2,1,0:T(8,128)(2,1)} %bitcast.68), calls=%async_computation.1 | async-start | bytes 8388608 | tf_op jit(solution)/shard_map/all_to_all | solution.py:36
  31.9 0.2 all-gather.2.cloned.1.call-start
  32.1 0.5 all-gather.2.cloned.1.call-update
  32.6 93.7 %all-to-all-done = bf16[16,64,2048]{2,1,0:T(8,128)(2,1)} async-done(((bf16[16,64,2048]{2,1,0:T(8,128)(2,1)}), bf16[16,64,2048]{2,1,0:T(8,128)(2,1)}, u32[]{:S(2)}, u32[]{:S(2)}) %all-to-all-start) | async-done | bytes 4194336 | tf_op jit(solution)/shard_map/all_to_all | solution.py:36
  126.3 11.7 %fusion.4 = f32[1024,1408]{1,0:T(8,128)} fusion(bf16[1024,2048]{1,0:T(8,128)(2,1)} %bitcast.5, bf16[1,2048,1408]{2,1,0:T(8,128)(2,1)} %param.13), kind=kOutput, calls=%fused_computation.6 | convolution fusion | flops 5905580032 | bytes 15728640 | tf_op jit(solution)/shard_map/dot_general | solution.py:8
  138.0 20.6 %fusion.10 = bf16[1024,2048]{1,0:T(8,128)(2,1)} fusion(bf16[1,1408,2048]{2,1,0:T(8,128)(2,1)} %param.15, f32[1024,1408]{1,0:T(8,128)} %fusion.4, bf16[1024,2048]{1,0:T(8,128)(2,1)} %bitcast.5, bf16[1,2048,1408]{2,1,0:T(8,128)(2,1)} %param.14), kind=kOutput, calls=%fused_computation.9 | convolution fusion | flops 11821907968 | bytes 25690112 | tf_op jit(solution)/shard_map/dot_general | solution.py:42
  158.7 5.3 %all-to-all-start.1 = ((bf16[16,64,2048]{2,1,0:T(8,128)(2,1)}), bf16[16,64,2048]{2,1,0:T(8,128)(2,1)}, u32[]{:S(2)}, u32[]{:S(2)}) async-start(bf16[16,64,2048]{2,1,0:T(8,128)(2,1)} %bitcast.69), calls=%async_computation.2 | async-start | bytes 8388608 | tf_op jit(solution)/shard_map/all_to_all | solution.py:44
  164.0 0.3 reduce-scatter.2.cloned.1.call-start
  164.3 0.0 all-gather.2.cloned.1.call-done
  164.3 5.2 %fusion.30 = f32[512,704]{0,1:T(8,128)} fusion(bf16[512,2048]{1,0:T(8,128)(2,1)} %all-gather.2.cloned.1.call-done, bf16[2048,704]{0,1:T(8,128)(2,1)} %param.16), kind=kOutput, calls=%fused_computation.37 | convolution fusion | flops 1476395008 | bytes 6422528 | tf_op jit(solution)/shard_map/dot_general | solution.py:8
  169.5 0.0 copy-done
  169.5 0.0 copy-start.3
  169.5 0.0 copy-start.2
  169.5 0.0 copy-start.1
  169.5 7.7 %convolution_convert_fusion = bf16[512,2048]{1,0:T(8,128)(2,1)} fusion(bf16[704,2048]{1,0:T(8,128)(2,1)S(1)} %copy-done, bf16[512,2048]{1,0:T(8,128)(2,1)} %all-gather.2.cloned.1.call-done, bf16[2048,704]{0,1:T(8,128)(2,1)} %param.17, f32[512,704]{0,1:T(8,128)} %fusion.30), kind=kOutput, calls=%fused_computation.10 | convolution fusion | flops 2956001280 | bytes 11403264 | tf_op jit(solution)/shard_map/dot_general | solution.py:49
  177.2 0.0 reduce-scatter.2.cloned.1.call-update
  177.2 0.0 copy-done.3
  177.3 0.2 copy.15
  177.4 0.0 copy-done.2
  177.5 0.0 copy-done.1
  177.5 0.2 fusion.22
  177.7 78.8 %all-to-all-done.1 = bf16[16,64,2048]{2,1,0:T(8,128)(2,1)} async-done(((bf16[16,64,2048]{2,1,0:T(8,128)(2,1)}), bf16[16,64,2048]{2,1,0:T(8,128)(2,1)}, u32[]{:S(2)}, u32[]{:S(2)}) %all-to-all-start.1) | async-done | bytes 4194336 | tf_op jit(solution)/shard_map/all_to_all | solution.py:44
  256.5 8.0 %gather_fusion = bf16[512,2048]{1,0:T(8,128)(2,1)} fusion(bf16[1024,2048]{1,0:T(8,128)(2,1)} %bitcast.10, s32[1024]{0:T(1024)S(1)} %pad_clamp_fusion), kind=kCustom, calls=%fused_computation | custom fusion | bytes 4196352 | tf_op jit(solution)/shard_map/gather | solution.py:45
  264.5 4.1 %reshape.71 = bf16[128,4,2048]{2,1,0:T(4,128)(2,1)} reshape(bf16[512,2048]{1,0:T(8,128)(2,1)} %gather_fusion) | data formatting | bytes 4194304 | tf_op jit(solution)/shard_map/reshape | solution.py:45
  268.6 3.9 %fusion.31 = f32[128,1,2048]{2,1,0:T(1,128)} fusion(bf16[128,4,2048]{2,1,0:T(4,128)(2,1)} %reshape.71, bf16[128,4,1]{1,2,0:T(2,128)(2,1)S(1)} %copy.15), kind=kOutput, calls=%fused_computation.38 | convolution fusion | flops 2097152 | bytes 3146752 | tf_op jit(solution)/shard_map/tk,tkd->td/dot_general | solution.py:46
  272.5 0.0 reduce-scatter.2.cloned.1.call-done
  272.5 2.6 fusion.23
  (6 shorter events, 0.1 us)
Async XLA Ops:
  6.5 163.0 %copy-start = (bf16[704,2048]{1,0:T(8,128)(2,1)S(1)}, bf16[704,2048]{1,0:T(8,128)(2,1)}, u32[]{:S(2)}) copy-start(bf16[704,2048]{1,0:T(8,128)(2,1)} %param.18) | copy-start | bytes 8650756
  24.7 101.6 %all-to-all-start = ((bf16[16,64,2048]{2,1,0:T(8,128)(2,1)}), bf16[16,64,2048]{2,1,0:T(8,128)(2,1)}, u32[]{:S(2)}, u32[]{:S(2)}) async-start(bf16[16,64,2048]{2,1,0:T(8,128)(2,1)} %bitcast.68), calls=%async_computation.1 | async-start | bytes 8388608 | tf_op jit(solution)/shard_map/all_to_all | solution.py:36
  31.9 132.4 %all-gather.2.cloned.1.call-start = ((), (), s32[]{:S(2)}) async-start(), calls=%async_computation.3 | async-start | bytes 2621440 | tf_op jit(solution)/shard_map/all_gather | solution.py:47
  158.7 97.8 %all-to-all-start.1 = ((bf16[16,64,2048]{2,1,0:T(8,128)(2,1)}), bf16[16,64,2048]{2,1,0:T(8,128)(2,1)}, u32[]{:S(2)}, u32[]{:S(2)}) async-start(bf16[16,64,2048]{2,1,0:T(8,128)(2,1)} %bitcast.69), calls=%async_computation.2 | async-start | bytes 8388608 | tf_op jit(solution)/shard_map/all_to_all | solution.py:44
  164.0 108.5 %reduce-scatter.2.cloned.1.call-start = ((), (), s32[]{:S(2)}) async-start(), calls=%async_computation.4 | async-start | bytes 2621440 | tf_op jit(solution)/shard_map/reduce_scatter | solution.py:48
  169.5 7.7 %copy-start.3 = (f32[128,4]{0,1:T(4,128)S(1)}, f32[128,4]{0,1:T(4,128)}, u32[]{:S(2)}) copy-start(f32[128,4]{0,1:T(4,128)} %param.12) | copy-start | bytes 6148
  169.5 7.9 %copy-start.2 = (bf16[2048]{0:T(1024)(128)(2,1)S(1)}, bf16[2048]{0:T(1024)(128)(2,1)}, u32[]{:S(2)}) copy-start(bf16[2048]{0:T(1024)(128)(2,1)} %param.19) | copy-start | bytes 12292
  169.5 7.9 %copy-start.1 = (bf16[128,2048]{1,0:T(8,128)(2,1)S(1)}, bf16[128,2048]{1,0:T(8,128)(2,1)}, u32[]{:S(2)}) copy-start(bf16[128,2048]{1,0:T(8,128)(2,1)} %param.10) | copy-start | bytes 1572868
Sparse Core Ops, SparseCore 0:
  34.5 62.7 all-gather.1
  177.4 61.1 reduce-scatter.1
where the time goes:
time: 283 us; the launch traced here: 282 us
  waiting for transfers between devices  173 us (61%)
  matrix products  49.4 us (17%)
  local copies, waits for them, and re-layouts  28.5 us (10%)
  between operations  13.5 us (5%)
  starting transfers between devices  12.9 us (5%)
  other arithmetic  4.58 us (2%)
    all_to_all x1, waiting for transfers between devices, per_device(): lax.all_to_all(outgoing, ('expert', 'tensor'), split_axis=0, concat_axis=...  93.7 us
    all_to_all x1, waiting for transfers between devices, per_device(): lax.all_to_all(finished, ('expert', 'tensor'), split_axis=0, concat_axis=...  78.8 us
    dot_general x1, matrix products, per_device(): jnp.dot(hidden, own_down, preferred_element_type=jnp.float32)  20.6 us
    dot_general x2, matrix products, silu_product(): gate = jnp.dot(rows, w_first, preferred_element_type=jnp.float32)  17 us
    gather x1, local copies, waits for them, and re-layouts, per_device(): back.reshape(experts * capacity, width)[slot].reshape(tok_dev, top, width)  8 us
    dot_general x1, matrix products, per_device(): jnp.dot(shared_hidden, s_down, preferred_element_type=jnp.float32)  7.68 us
    scatter x1, local copies, waits for them, and re-layouts, per_device(): jnp.zeros((experts * capacity, width), jnp.bfloat16).at[slot].set(repeated)  7.21 us
    all_to_all x1, starting transfers between devices, per_device(): lax.all_to_all(outgoing, ('expert', 'tensor'), split_axis=0, concat_axis=...  7.14 us
  transfers between devices with their start and end apart: 4, of which 2 were waited for; matrix products, arithmetic and copies ran while one was open for 22% of the time, Pallas kernels for 0%

commit v1 on v0

v1 whole, which is shorter than its diff:
```python
import functools

import jax
import jax.numpy as jnp
from jax import lax
from jax.experimental import pallas as pl
from jax.experimental.pallas import tpu as pltpu
from jax.sharding import PartitionSpec as P

MESH = pl.DeviceIdType.MESH
BF = jnp.bfloat16
F32 = jnp.float32


def partner(index, step, size):
    total, bit = 0, 1
    while bit < size:
        total = total + ((index // bit + step // bit) % 2) * bit
        bit *= 2
    return total


def pieces(extent, width):
    return [(start, min(width, extent - start)) for start in range(0, extent, width)]


def layer_kernel(
    ne, nt, cap,
    tok_hbm, ids_ref, prob_ref, wg_hbm, wu_hbm, wd_hbm, sg_hbm, su_hbm, sd_hbm, gate_ref,
    out_ref,
    wg, wu, wd, sg, su, sd,
    meta, meta_z, meta_t,
    tok_t, tok_z, rows, stage, back, back_t, back_z, hidden, hidden_s, part_s, total,
    load_sem, mz_send, mz_recv, mt_send, mt_recv, tz_send, tz_recv, tt_send, tt_recv,
    d_send, d_recv, r_send, r_recv, bt_send, bt_recv, bz_send, bz_recv,
):
    tok, width = out_ref.shape
    top = ids_ref.shape[0]
    experts = ne * nt
    z = lax.axis_index("expert")
    t = lax.axis_index("tensor")

    def remote(src, dst, send, recv, axis, peer):
        return pltpu.make_async_remote_copy(
            src_ref=src, dst_ref=dst, send_sem=send, recv_sem=recv,
            device_id={axis: peer}, device_id_type=MESH,
        )

    def z_peer(s):
        return partner(z, s, ne)

    def t_peer(k):
        return partner(t, k, nt)

    tok_load = pltpu.make_async_copy(tok_hbm, tok_t.at[0], load_sem.at[0])
    tok_load.start()
    barrier = pltpu.get_barrier_semaphore()
    for s in range(1, ne):
        pl.semaphore_signal(barrier, inc=1, device_id={"expert": z_peer(s)}, device_id_type=MESH)
    for k in range(1, nt):
        pl.semaphore_signal(barrier, inc=1, device_id={"tensor": t_peer(k)}, device_id_type=MESH)
    loads = [
        pltpu.make_async_copy(src, dst, load_sem.at[1 + i])
        for i, (src, dst) in enumerate(
            ((sg_hbm, sg), (su_hbm, su), (sd_hbm, sd),
             (wg_hbm.at[0], wg), (wu_hbm.at[0], wu), (wd_hbm.at[0], wd))
        )
    ]

    number = lax.broadcasted_iota(jnp.int32, (experts, tok), 0)
    weight = jnp.zeros((experts, tok), F32)
    chosen = jnp.zeros((experts, tok), F32)
    for k in range(top):
        hit = ids_ref[k:k + 1, :] == number
        weight = weight + jnp.where(hit, prob_ref[k:k + 1, :], 0.0)
        chosen = chosen + jnp.where(hit, 1.0, 0.0)
    earlier = lax.broadcasted_iota(jnp.int32, (tok, tok), 0) < lax.broadcasted_iota(jnp.int32, (tok, tok), 1)
    rank = jnp.dot(chosen.astype(BF), jnp.where(earlier, 1.0, 0.0).astype(BF), preferred_element_type=F32)
    place = jnp.where(chosen > 0.0, rank, -1.0)
    for e in range(ne):
        meta[e, 0:nt, :] = place[e * nt:(e + 1) * nt]
        meta[e, nt:2 * nt, :] = weight[e * nt:(e + 1) * nt]

    def meta_z_copy(s):
        return remote(meta.at[z_peer(s)], meta_z.at[s], mz_send.at[s], mz_recv.at[s], "expert", z_peer(s))

    def meta_t_copy(k):
        return remote(meta.at[z], meta_t.at[k], mt_send.at[k], mt_recv.at[k], "tensor", t_peer(k))

    def tok_z_copy(s):
        return remote(tok_t.at[0], tok_z.at[s], tz_send.at[s], tz_recv.at[s], "expert", z_peer(s))

    def tok_t_copy(k):
        return remote(tok_t.at[0], tok_t.at[k], tt_send.at[k], tt_recv.at[k], "tensor", t_peer(k))

    def dispatch_copy(s, k):
        return remote(
            stage.at[s, pl.ds(k * cap, cap)], rows.at[s, pl.ds(k * cap, cap)],
            d_send.at[s, k], d_recv.at[s, k], "tensor", t_peer(k),
        )

    def return_copy(s, k):
        return remote(
            rows.at[s, pl.ds(k * cap, cap)], back.at[s, pl.ds(k * cap, cap)],
            r_send.at[s, k], r_recv.at[s, k], "tensor", t_peer(k),
        )

    def back_t_copy(k):
        return remote(tok_t.at[k], back_t.at[k], bt_send.at[k], bt_recv.at[k], "tensor", t_peer(k))

    def back_z_copy(s):
        return remote(tok_z.at[s], back_z.at[s], bz_send.at[s], bz_recv.at[s], "expert", z_peer(s))

    tok_load.wait()
    pl.semaphore_wait(barrier, ne - 1 + nt - 1)
    for s in range(1, ne):
        meta_z_copy(s).start()
    for k in range(1, nt):
        meta_t_copy(k).start()
    for s in range(1, ne):
        tok_z_copy(s).start()
    for k in range(1, nt):
        tok_t_copy(k).start()
    for load in loads:
        load.start()
    meta_t[0] = meta[z]

    slots = lax.broadcasted_iota(jnp.int32, (cap, tok), 0).astype(F32)

    def picker(place_row):
        return jnp.where(slots == place_row, 1.0, 0.0).astype(BF)

    def weigher(place_row, weight_row):
        return jnp.where(slots == place_row, weight_row, 0.0).astype(BF)

    def dispatch(s):
        meta_z_copy(s).wait_recv()
        tok_z_copy(s).wait_recv()
        for k in [*range(1, nt), 0]:
            pick = picker(meta_z[s, pl.ds(t_peer(k), 1), :])
            span = pl.ds(k * cap, cap)
            for c, w in pieces(width, 512):
                got = jnp.dot(pick, tok_z[s, :, c:c + w], preferred_element_type=F32).astype(BF)
                if k:
                    stage[s, span, c:c + w] = got
                else:
                    rows[s, span, c:c + w] = got
            if k:
                dispatch_copy(s, k).start()

    def expert(s):
        for c, w in pieces(wg.shape[1], 256):
            x = rows[s]
            g = jnp.dot(x, wg[:, c:c + w], preferred_element_type=F32)
            u = jnp.dot(x, wu[:, c:c + w], preferred_element_type=F32)
            hidden[:, c:c + w] = (g / (1.0 + jnp.exp(-g)) * u).astype(BF)
        for c, w in pieces(width, 256):
            rows[s, :, c:c + w] = jnp.dot(hidden[...], wd[:, c:c + w], preferred_element_type=F32).astype(BF)

    def each(first, last, body):
        def step(i, carry):
            body(i)
            return carry
        lax.fori_loop(first, last, step, 0)

    early = min(ne, ne // 2 + 1)
    each(1, early, dispatch)

    for k in range(1, nt):
        tok_t_copy(k).wait_recv()
        meta_t_copy(k).wait_recv()
    for load in loads[:3]:
        load.wait()
    nk = (((1,), (1,)), ((), ()))
    all_rows = nt * tok
    for c, w in pieces(sg.shape[0], 256):
        x = tok_t[...].reshape(all_rows, width)
        g = lax.dot_general(x, sg[c:c + w, :], nk, preferred_element_type=F32)
        u = lax.dot_general(x, su[c:c + w, :], nk, preferred_element_type=F32)
        hidden_s[:, c:c + w] = (g / (1.0 + jnp.exp(-g)) * u).astype(BF)
    for c, w in pieces(width, 256):
        part_s[:, c:c + w] = jnp.dot(hidden_s[...], sd[:, c:c + w], preferred_element_type=F32).astype(BF)

    each(early, ne, dispatch)

    for load in loads[3:]:
        load.wait()
    for k in range(nt):
        pick = picker(meta_t[k, pl.ds(t, 1), :])
        for c, w in pieces(width, 512):
            rows[0, k * cap:(k + 1) * cap, c:c + w] = jnp.dot(
                pick, tok_t[k, :, c:c + w], preferred_element_type=F32).astype(BF)

    def routed_stage(i):
        s = (i + 1) % (ne - 1) + 1 if ne > 2 else i + 1
        s = jnp.where(i == ne - 1, 0, s)
        last = i == ne - 1

        @pl.when(jnp.logical_not(last))
        def _():
            for k in range(1, nt):
                dispatch_copy(s, k).wait_recv()

        expert(s)

        @pl.when(jnp.logical_not(last))
        def _():
            for k in range(1, nt):
                return_copy(s, k).start()
            back[s, 0:cap] = rows[s, 0:cap]

    each(0, ne, routed_stage)

    flip = (((0,), (0,)), ((), ()))
    for k in range(1, nt):
        tok_t_copy(k).wait_send()
    for s in range(1, ne):
        tok_z_copy(s).wait_send()
    for k in [*range(1, nt), 0]:
        part = weigher(meta_t[k, pl.ds(t, 1), :], meta_t[k, pl.ds(nt + t, 1), :])
        logit = jnp.sum(tok_t[k].astype(F32) * gate_ref[...].astype(F32), axis=1, keepdims=True)
        scale = 1.0 / (1.0 + jnp.exp(-logit))
        for c, w in pieces(width, 512):
            got = lax.dot_general(part, rows[0, k * cap:(k + 1) * cap, c:c + w], flip, preferred_element_type=F32)
            got = got + scale * part_s[k * tok:(k + 1) * tok, c:c + w].astype(F32)
            if k:
                tok_t[k, :, c:c + w] = got.astype(BF)
            else:
                total[:, c:c + w] = got
        if k:
            back_t_copy(k).start()

    def combine(i):
        s = (i + 1) % (ne - 1) + 1 if ne > 2 else i + 1
        for k in range(1, nt):
            return_copy(s, k).wait_recv()
        parts = jnp.concatenate(
            [weigher(meta_z[s, pl.ds(t_peer(k), 1), :], meta_z[s, pl.ds(nt + t_peer(k), 1), :]) for k in range(nt)],
            axis=0,
        )
        for c, w in pieces(width, 512):
            tok_z[s, :, c:c + w] = lax.dot_general(
                parts, back[s, :, c:c + w], flip, preferred_element_type=F32).astype(BF)
        back_z_copy(s).start()

    each(0, ne - 1, combine)
    for s in range(1, ne):
        back_z_copy(s).wait_recv()
        total[...] += back_z[s].astype(F32)
    for k in range(1, nt):
        back_t_copy(k).wait_recv()
        total[...] += back_t[k].astype(F32)
    out_ref[...] = total[...].astype(BF)

    for s in range(1, ne):
        meta_z_copy(s).wait_send()
        back_z_copy(s).wait_send()
        for k in range(1, nt):
            dispatch_copy(s, k).wait_send()
            return_copy(s, k).wait_send()
    for k in range(1, nt):
        meta_t_copy(k).wait_send()
        back_t_copy(k).wait_send()


def per_device(
    tokens, expert_ids, gate_probs, w_gate, w_up, w_down, s_gate, s_up, s_down, shared_gate
):
    tok, width = tokens.shape
    top = expert_ids.shape[1]
    ne = lax.axis_size("expert")
    nt = lax.axis_size("tensor")
    experts = ne * nt
    cap = max(2, 2 * top * tok // experts)
    inner = w_gate.shape[2]
    inner_s = s_gate.shape[1]
    vmem = pl.BlockSpec(memory_space=pltpu.VMEM)
    hbm = pl.BlockSpec(memory_space=pl.ANY)
    dma = pltpu.SemaphoreType.DMA
    group = nt * cap
    return pl.pallas_call(
        functools.partial(layer_kernel, ne, nt, cap),
        out_shape=jax.ShapeDtypeStruct((tok, width), BF),
        in_specs=[hbm, vmem, vmem, hbm, hbm, hbm, hbm, hbm, hbm, vmem],
        out_specs=vmem,
        scratch_shapes=[
            pltpu.VMEM((width, inner), BF),
            pltpu.VMEM((width, inner), BF),
            pltpu.VMEM((inner, width), BF),
            pltpu.VMEM((inner_s, width), BF),
            pltpu.VMEM((inner_s, width), BF),
            pltpu.VMEM((inner_s, width), BF),
            pltpu.VMEM((ne, 2 * nt, tok), F32),
            pltpu.VMEM((ne, 2 * nt, tok), F32),
            pltpu.VMEM((nt, 2 * nt, tok), F32),
            pltpu.VMEM((nt, tok, width), BF),
            pltpu.VMEM((ne, tok, width), BF),
            pltpu.VMEM((ne, group, width), BF),
            pltpu.VMEM((ne, group, width), BF),
            pltpu.VMEM((ne, group, width), BF),
            pltpu.VMEM((nt, tok, width), BF),
            pltpu.VMEM((ne, tok, width), BF),
            pltpu.VMEM((group, inner), BF),
            pltpu.VMEM((nt * tok, inner_s), BF),
            pltpu.VMEM((nt * tok, width), BF),
            pltpu.VMEM((tok, width), F32),
            dma((7,)),
            dma((ne,)), dma((ne,)), dma((nt,)), dma((nt,)),
            dma((ne,)), dma((ne,)), dma((nt,)), dma((nt,)),
            dma((ne, nt)), dma((ne, nt)), dma((ne, nt)), dma((ne, nt)),
            dma((nt,)), dma((nt,)), dma((ne,)), dma((ne,)),
        ],
        compiler_params=pltpu.CompilerParams(
            collective_id=0, has_side_effects=True, vmem_limit_bytes=67043328
        ),
        name="moe_layer",
    )(
        tokens, expert_ids.T, gate_probs.T, w_gate, w_up, w_down,
        s_gate.T, s_up.T, s_down, shared_gate.reshape(1, width),
    )


def solution(mesh):
    return jax.shard_map(
        per_device,
        mesh=mesh,
        in_specs=(
            P(("dp", "expert", "tensor"), None),
            P(("dp", "expert", "tensor"), None),
            P(("dp", "expert", "tensor"), None),
            P(("expert", "tensor"), None, None),
            P(("expert", "tensor"), None, None),
            P(("expert", "tensor"), None, None),
            P(None, "tensor"),
            P(None, "tensor"),
            P("tensor", None),
            P(),
        ),
        out_specs=P(("dp", "expert", "tensor"), None),
        check_vma=False,
    )
```

time: 283 us -> 132 us (0.47)
  the two profiles are of different devices: /device:TPU:14 before, /device:TPU:0 now
where the time goes in v1:
time: 132 us
  Pallas kernels  129 us (98%)
  local copies, waits for them, and re-layouts  3.17 us (2%)
    pallas_call x1, Pallas kernels, per_device(): pl.pallas_call(functools.partial(layer_kernel, ne, nt, cap), out_shape=ja...  129 us

profile of v1, /device:TPU:0, one launch (start us, length us, event | category | flops | bytes accessed | tf_op | source)
XLA Modules:
  0.0 131.9 jit_solution(3458363632170639502)
XLA Ops:
  0.0 1.3 reshape.3.gate_ref
  1.3 128.8 %moe_layer.1 = bf16[128,2048]{1,0:T(8,128)(2,1)} custom-call(bf16[128,2048]{1,0:T(8,128)(2,1)} %tok_hbm.1, s32[4,128]{1,0:T(4,128)} %bitcast.6, f32[4,128]{1,0:T(4,128)} %bitcast.7, bf16[1,2048,1408]{2,1,0:T(8,128)(2,1)} %wg_hbm.1, bf16[1,2048,1408]{2,1,0:T(8,128)(2,1)} %wu_hbm.1, bf16[1,1408,2048]{2,1,0:T(8,128)(2,1)} %wd_hbm.1, bf16[704,2048]{1,0:T(8,128)(2,1)} %bitcast.4, ...), custom_call_target="tpu_custom_call" | custom-call | tf_op jit(solution)/shard_map/moe_layer/pallas_call | solution.py:281
  130.1 1.9 %copy.12 = bf16[128,2048]{1,0:T(8,128)(2,1)} copy(bf16[128,2048]{1,0:T(8,128)(2,1)} %moe_layer.1) | data formatting | bytes 1048576

commit v2 on v1

--- a/solution.py
+++ b/solution.py
@@ -30,7 +30,7 @@
     out_ref,
     wg, wu, wd, sg, su, sd,
     meta, meta_z, meta_t,
-    tok_t, tok_z, rows, stage, back, back_t, back_z, hidden, hidden_s, part_s, total,
+    tok_t, tok_z, rows, stage, back, back_t, back_z, hidden, hidden_s, part_s, total, held,
     load_sem, mz_send, mz_recv, mt_send, mt_recv, tz_send, tz_recv, tt_send, tt_recv,
     d_send, d_recv, r_send, r_recv, bt_send, bt_recv, bz_send, bz_recv,
 ):
@@ -85,13 +85,40 @@
         return remote(meta.at[z_peer(s)], meta_z.at[s], mz_send.at[s], mz_recv.at[s], "expert", z_peer(s))
 
     def meta_t_copy(k):
-        return remote(meta.at[z], meta_t.at[k], mt_send.at[k], mt_recv.at[k], "tensor", t_peer(k))
+        return remote(meta, meta_t.at[k], mt_send.at[k], mt_recv.at[k], "tensor", t_peer(k))
 
     def tok_z_copy(s):
         return remote(tok_t.at[0], tok_z.at[s], tz_send.at[s], tz_recv.at[s], "expert", z_peer(s))
 
-    def tok_t_copy(k):
-        return remote(tok_t.at[0], tok_t.at[k], tt_send.at[k], tt_recv.at[k], "tensor", t_peer(k))
+    def forward_copy(s):
+        return remote(tok_z.at[s - 1], tok_z.at[s], tz_send.at[s], tz_recv.at[s], "expert", z_peer(1))
+
+    half = tok // 2
+    relayed = nt == 4
+
+    def part_rows(h):
+        return pl.ds(h * half, half)
+
+    def tok_t_copy(k, h):
+        return remote(
+            tok_t.at[0, part_rows(h)], tok_t.at[k, part_rows(h)],
+            tt_send.at[k, h], tt_recv.at[k, h], "tensor", t_peer(k),
+        )
+
+    def relay_copy(h):
+        return remote(
+            tok_t.at[2 - h, part_rows(h)], tok_t.at[3, part_rows(h)],
+            tt_send.at[3, h], tt_recv.at[3, h], "tensor", t_peer(1 + h),
+        )
+
+    def near_copy(k):
+        return remote(
+            stage.at[1, pl.ds(k * cap, cap)], rows.at[1, pl.ds(k * cap, cap)],
+            d_send.at[1, k], d_recv.at[1, k], "expert", z_peer(1),
+        )
+
+    def near_back_copy():
+        return remote(rows.at[1], back.at[1], r_send.at[1, 0], r_recv.at[1, 0], "expert", z_peer(1))
 
     def dispatch_copy(s, k):
         return remote(
@@ -105,25 +132,46 @@
             r_send.at[s, k], r_recv.at[s, k], "tensor", t_peer(k),
         )
 
-    def back_t_copy(k):
-        return remote(tok_t.at[k], back_t.at[k], bt_send.at[k], bt_recv.at[k], "tensor", t_peer(k))
+    def back_t_copy(k, h):
+        return remote(
+            tok_t.at[k, part_rows(h)], back_t.at[k, part_rows(h)],
+            bt_send.at[k, h], bt_recv.at[k, h], "tensor", t_peer(k),
+        )
+
+    def back_relay_copy(h):
+        return remote(
+            tok_t.at[3, part_rows(h)], back_t.at[3, part_rows(h)],
+            bt_send.at[3, h], bt_recv.at[3, h], "tensor", t_peer(1 + h),
+        )
 
     def back_z_copy(s):
         return remote(tok_z.at[s], back_z.at[s], bz_send.at[s], bz_recv.at[s], "expert", z_peer(s))
 
+    def back_near_copy(s):
+        return remote(tok_z.at[s], back_z.at[s], bz_send.at[s], bz_recv.at[s], "expert", z_peer(1))
+
+    def each(first, last, body):
+        def step(i, carry):
+            body(i)
+            return carry
+        lax.fori_loop(first, last, step, 0)
+
+    direct = [(2, 0), (1, 1), (2, 1), (1, 0)] if relayed else [(k, h) for k in range(1, nt) for h in range(2)]
+    peers = sorted({k for k, _ in direct})
+
     tok_load.wait()
     pl.semaphore_wait(barrier, ne - 1 + nt - 1)
-    for s in range(1, ne):
-        meta_z_copy(s).start()
+    for k, h in direct:
+        tok_t_copy(k, h).start()
+    for s in range(2, ne, 2):
+        tok_z_copy(s).start()
     for k in range(1, nt):
         meta_t_copy(k).start()
-    for s in range(1, ne):
-        tok_z_copy(s).start()
-    for k in range(1, nt):
-        tok_t_copy(k).start()
+    for s in range(2, ne):
+        meta_z_copy(s).start()
     for load in loads:
         load.start()
-    meta_t[0] = meta[z]
+    meta_t[0] = meta[...]
 
     slots = lax.broadcasted_iota(jnp.int32, (cap, tok), 0).astype(F32)
 
@@ -133,9 +181,14 @@
     def weigher(place_row, weight_row):
         return jnp.where(slots == place_row, weight_row, 0.0).astype(BF)
 
+    def near(k):
+        pick = picker(meta_t[k, z_peer(1), pl.ds(t, 1), :])
+        for c, w in pieces(width, 512):
+            stage[1, k * cap:(k + 1) * cap, c:c + w] = jnp.dot(
+                pick, tok_t[k, :, c:c + w], preferred_element_type=F32).astype(BF)
+        near_copy(k).start()
+
     def dispatch(s):
-        meta_z_copy(s).wait_recv()
-        tok_z_copy(s).wait_recv()
         for k in [*range(1, nt), 0]:
             pick = picker(meta_z[s, pl.ds(t_peer(k), 1), :])
             span = pl.ds(k * cap, cap)
@@ -148,6 +201,19 @@
             if k:
                 dispatch_copy(s, k).start()
 
+    def dispatch_even(j):
+        s = 2 * j
+        tok_z_copy(s).wait_recv()
+        forward_copy(s + 1).start()
+        meta_z_copy(s).wait_recv()
+        dispatch(s)
+
+    def dispatch_odd(j):
+        s = 2 * j + 1
+        forward_copy(s).wait_recv()
+        meta_z_copy(s).wait_recv()
+        dispatch(s)
+
     def expert(s):
         for c, w in pieces(wg.shape[1], 256):
             x = rows[s]
@@ -157,18 +223,27 @@
         for c, w in pieces(width, 256):
             rows[s, :, c:c + w] = jnp.dot(hidden[...], wd[:, c:c + w], preferred_element_type=F32).astype(BF)
 
-    def each(first, last, body):
-        def step(i, carry):
-            body(i)
-            return carry
-        lax.fori_loop(first, last, step, 0)
-
-    early = min(ne, ne // 2 + 1)
-    each(1, early, dispatch)
-
+    near(0)
+    if relayed:
+        tok_t_copy(2, 0).wait_recv()
+        relay_copy(0).start()
+        tok_t_copy(1, 1).wait_recv()
+        relay_copy(1).start()
+        rest = [(2, 1), (1, 0)]
+    else:
+        rest = direct
+    for k, h in rest:
+        tok_t_copy(k, h).wait_recv()
     for k in range(1, nt):
-        tok_t_copy(k).wait_recv()
         meta_t_copy(k).wait_recv()
+    for k in peers:
+        near(k)
+    each(1, ne // 2, dispatch_even)
+    if relayed:
+        for h in range(2):
+            relay_copy(h).wait_recv()
+        near(3)
+
     for load in loads[:3]:
         load.wait()
     nk = (((1,), (1,)), ((), ()))
@@ -178,32 +253,43 @@
         g = lax.dot_general(x, sg[c:c + w, :], nk, preferred_element_type=F32)
         u = lax.dot_general(x, su[c:c + w, :], nk, preferred_element_type=F32)
         hidden_s[:, c:c + w] = (g / (1.0 + jnp.exp(-g)) * u).astype(BF)
+
+    each(1, ne // 2, dispatch_odd)
+
     for c, w in pieces(width, 256):
         part_s[:, c:c + w] = jnp.dot(hidden_s[...], sd[:, c:c + w], preferred_element_type=F32).astype(BF)
-
-    each(early, ne, dispatch)
 
     for load in loads[3:]:
         load.wait()
     for k in range(nt):
-        pick = picker(meta_t[k, pl.ds(t, 1), :])
+        pick = picker(meta_t[k, z, pl.ds(t, 1), :])
         for c, w in pieces(width, 512):
             rows[0, k * cap:(k + 1) * cap, c:c + w] = jnp.dot(
                 pick, tok_t[k, :, c:c + w], preferred_element_type=F32).astype(BF)
 
     def routed_stage(i):
-        s = (i + 1) % (ne - 1) + 1 if ne > 2 else i + 1
+        pairs = ne // 2
+        s = jnp.where(i < pairs - 1, 2 * i + 2, 2 * (i - pairs) + 3)
+        s = jnp.where(i == pairs - 1, 1, s)
         s = jnp.where(i == ne - 1, 0, s)
-        last = i == ne - 1
-
-        @pl.when(jnp.logical_not(last))
+
+        @pl.when(s == 1)
+        def _():
+            for k in range(nt):
+                near_copy(k).wait_recv()
+
+        @pl.when(s > 1)
         def _():
             for k in range(1, nt):
                 dispatch_copy(s, k).wait_recv()
 
         expert(s)
 
-        @pl.when(jnp.logical_not(last))
+        @pl.when(s == 1)
+        def _():
+            near_back_copy().start()
+
+        @pl.when(s > 1)
         def _():
             for k in range(1, nt):
                 return_copy(s, k).start()
@@ -212,55 +298,107 @@
     each(0, ne, routed_stage)
 
     flip = (((0,), (0,)), ((), ()))
-    for k in range(1, nt):
-        tok_t_copy(k).wait_send()
-    for s in range(1, ne):
-        tok_z_copy(s).wait_send()
-    for k in [*range(1, nt), 0]:
-        part = weigher(meta_t[k, pl.ds(t, 1), :], meta_t[k, pl.ds(nt + t, 1), :])
-        logit = jnp.sum(tok_t[k].astype(F32) * gate_ref[...].astype(F32), axis=1, keepdims=True)
-        scale = 1.0 / (1.0 + jnp.exp(-logit))
-        for c, w in pieces(width, 512):
-            got = lax.dot_general(part, rows[0, k * cap:(k + 1) * cap, c:c + w], flip, preferred_element_type=F32)
-            got = got + scale * part_s[k * tok:(k + 1) * tok, c:c + w].astype(F32)
-            if k:
-                tok_t[k, :, c:c + w] = got.astype(BF)
-            else:
-                total[:, c:c + w] = got
-        if k:
-            back_t_copy(k).start()
-
-    def combine(i):
-        s = (i + 1) % (ne - 1) + 1 if ne > 2 else i + 1
+
+    def combined(s):
         for k in range(1, nt):
             return_copy(s, k).wait_recv()
-        parts = jnp.concatenate(
+        return jnp.concatenate(
             [weigher(meta_z[s, pl.ds(t_peer(k), 1), :], meta_z[s, pl.ds(nt + t_peer(k), 1), :]) for k in range(nt)],
             axis=0,
         )
+
+    def combine_odd(j):
+        s = 2 * j + 1
+        parts = combined(s)
         for c, w in pieces(width, 512):
             tok_z[s, :, c:c + w] = lax.dot_general(
                 parts, back[s, :, c:c + w], flip, preferred_element_type=F32).astype(BF)
+        back_near_copy(s).start()
+
+    def combine_even(j):
+        s = 2 * j
+        parts = combined(s)
+        forward_copy(s + 1).wait_send()
+        back_near_copy(s + 1).wait_recv()
+        for c, w in pieces(width, 512):
+            got = lax.dot_general(parts, back[s, :, c:c + w], flip, preferred_element_type=F32)
+            tok_z[s, :, c:c + w] = (got + back_z[s + 1, :, c:c + w].astype(F32)).astype(BF)
         back_z_copy(s).start()
 
-    each(0, ne - 1, combine)
-    for s in range(1, ne):
+    each(1, ne // 2, combine_odd)
+
+    for k, h in direct:
+        tok_t_copy(k, h).wait_send()
+    if relayed:
+        for h in range(2):
+            relay_copy(h).wait_send()
+    near_back_copy().wait_recv()
+
+    for k in ([3, 1, 2, 0] if relayed else [*range(1, nt), 0]):
+        own = weigher(meta_t[k, z, pl.ds(t, 1), :], meta_t[k, z, pl.ds(nt + t, 1), :])
+        by = z_peer(1)
+        other = weigher(meta_t[k, by, pl.ds(t, 1), :], meta_t[k, by, pl.ds(nt + t, 1), :])
+        logit = jnp.sum(tok_t[k].astype(F32) * gate_ref[...].astype(F32), axis=1, keepdims=True)
+        scale = 1.0 / (1.0 + jnp.exp(-logit))
+        span = slice(k * cap, (k + 1) * cap)
+        for c, w in pieces(width, 512):
+            got = lax.dot_general(own, rows[0, span, c:c + w], flip, preferred_element_type=F32)
+            got = got + lax.dot_general(other, back[1, span, c:c + w], flip, preferred_element_type=F32)
+            got = got + scale * part_s[k * tok:(k + 1) * tok, c:c + w].astype(F32)
+            if k == 0:
+                total[:, c:c + w] = got
+            elif relayed and k < 3:
+                now = slice((1 - k % 2) * half, (2 - k % 2) * half)
+                later = slice((k % 2) * half, (k % 2 + 1) * half)
+                tok_t[k, now, c:c + w] = got[now].astype(BF)
+                held[k, :, c:c + w] = got[later]
+            else:
+                tok_t[k, :, c:c + w] = got.astype(BF)
+        if relayed and k == 3:
+            for h in range(2):
+                back_relay_copy(h).start()
+        elif relayed and k:
+            back_t_copy(k, 1 - k % 2).start()
+        elif k:
+            for h in range(2):
+                back_t_copy(k, h).start()
+    if relayed:
+        for k in (1, 2):
+            h = k % 2
+            back_relay_copy(h).wait_recv()
+            tok_t[k, part_rows(h), :] = (held[k] + back_t[3, part_rows(h), :].astype(F32)).astype(BF)
+            back_t_copy(k, h).start()
+
+    each(1, ne // 2, combine_even)
+
+    for k in peers:
+        for h in range(2):
+            back_t_copy(k, h).wait_recv()
+        total[...] += back_t[k].astype(F32)
+    for s in range(2, ne, 2):
         back_z_copy(s).wait_recv()
         total[...] += back_z[s].astype(F32)
-    for k in range(1, nt):
-        back_t_copy(k).wait_recv()
-        total[...] += back_t[k].astype(F32)
     out_ref[...] = total[...].astype(BF)
 
-    for s in range(1, ne):
+    for k in range(nt):
+        near_copy(k).wait_send()
+    near_back_copy().wait_send()
+    for s in range(2, ne):
         meta_z_copy(s).wait_send()
-        back_z_copy(s).wait_send()
         for k in range(1, nt):
             dispatch_copy(s, k).wait_send()
             return_copy(s, k).wait_send()
+    for s in range(2, ne, 2):
+        tok_z_copy(s).wait_send()
+        back_z_copy(s).wait_send()
+        back_near_copy(s + 1).wait_send()
     for k in range(1, nt):
         meta_t_copy(k).wait_send()
-        back_t_copy(k).wait_send()
+    for k, h in direct:
+        back_t_copy(k, h).wait_send()
+    if relayed:
+        for h in range(2):
+            back_relay_copy(h).wait_send()
 
 
 def per_device(
@@ -292,7 +430,7 @@
             pltpu.VMEM((inner_s, width), BF),
             pltpu.VMEM((ne, 2 * nt, tok), F32),
             pltpu.VMEM((ne, 2 * nt, tok), F32),
-            pltpu.VMEM((nt, 2 * nt, tok), F32),
+            pltpu.VMEM((nt, ne, 2 * nt, tok), F32),
             pltpu.VMEM((nt, tok, width), BF),
             pltpu.VMEM((ne, tok, width), BF),
             pltpu.VMEM((ne, group, width), BF),
@@ -304,11 +442,12 @@
             pltpu.VMEM((nt * tok, inner_s), BF),
             pltpu.VMEM((nt * tok, width), BF),
             pltpu.VMEM((tok, width), F32),
+            pltpu.VMEM((3, tok // 2, width), F32),
             dma((7,)),
             dma((ne,)), dma((ne,)), dma((nt,)), dma((nt,)),
-            dma((ne,)), dma((ne,)), dma((nt,)), dma((nt,)),
+            dma((ne,)), dma((ne,)), dma((nt, 2)), dma((nt, 2)),
             dma((ne, nt)), dma((ne, nt)), dma((ne, nt)), dma((ne, nt)),
-            dma((nt,)), dma((nt,)), dma((ne,)), dma((ne,)),
+            dma((nt, 2)), dma((nt, 2)), dma((ne,)), dma((ne,)),
         ],
         compiler_params=pltpu.CompilerParams(
             collective_id=0, has_side_effects=True, vmem_limit_bytes=67043328

time: 132 us -> 130 us (0.985)
  Pallas kernels: 129 us -> 126 us
    pallas_call x1, Pallas kernels: 129 us -> 126 us  [per_device(): pl.pallas_call(functools.partial(layer_kernel, ne, nt, cap), out_shape=ja...]
where the time goes in v2:
time: 130 us; the launch traced here: 129 us
  Pallas kernels  126 us (97%)
  local copies, waits for them, and re-layouts  3.17 us (2%)
    pallas_call x1, Pallas kernels, per_device(): pl.pallas_call(functools.partial(layer_kernel, ne, nt, cap), out_shape=ja...  126 us

profile of v2, /device:TPU:0, one launch (start us, length us, event | category | flops | bytes accessed | tf_op | source)
XLA Modules:
  0.0 129.3 jit_solution(8468105674122254794)
XLA Ops:
  0.0 1.3 reshape.3.gate_ref
  1.3 126.2 %moe_layer.1 = bf16[128,2048]{1,0:T(8,128)(2,1)} custom-call(bf16[128,2048]{1,0:T(8,128)(2,1)} %tok_hbm.1, s32[4,128]{1,0:T(4,128)} %bitcast.6, f32[4,128]{1,0:T(4,128)} %bitcast.7, bf16[1,2048,1408]{2,1,0:T(8,128)(2,1)} %wg_hbm.1, bf16[1,2048,1408]{2,1,0:T(8,128)(2,1)} %wu_hbm.1, bf16[1,1408,2048]{2,1,0:T(8,128)(2,1)} %wd_hbm.1, bf16[704,2048]{1,0:T(8,128)(2,1)} %bitcast.4, ...), custom_call_target="tpu_custom_call" | custom-call | tf_op jit(solution)/shard_map/moe_layer/pallas_call | solution.py:419
  127.5 1.9 %copy.12 = bf16[128,2048]{1,0:T(8,128)(2,1)} copy(bf16[128,2048]{1,0:T(8,128)(2,1)} %moe_layer.1) | data formatting | bytes 1048576

commit v3 on v2

--- a/solution.py
+++ b/solution.py
@@ -111,12 +111,6 @@
             tt_send.at[3, h], tt_recv.at[3, h], "tensor", t_peer(1 + h),
         )
 
-    def near_copy(k):
-        return remote(
-            stage.at[1, pl.ds(k * cap, cap)], rows.at[1, pl.ds(k * cap, cap)],
-            d_send.at[1, k], d_recv.at[1, k], "expert", z_peer(1),
-        )
-
     def near_back_copy():
         return remote(rows.at[1], back.at[1], r_send.at[1, 0], r_recv.at[1, 0], "expert", z_peer(1))
 
@@ -144,11 +138,20 @@
             bt_send.at[3, h], bt_recv.at[3, h], "tensor", t_peer(1 + h),
         )
 
-    def back_z_copy(s):
-        return remote(tok_z.at[s], back_z.at[s], bz_send.at[s], bz_recv.at[s], "expert", z_peer(s))
-
-    def back_near_copy(s):
-        return remote(tok_z.at[s], back_z.at[s], bz_send.at[s], bz_recv.at[s], "expert", z_peer(1))
+    def columns(h):
+        return pl.ds(h * (width // 2), width // 2)
+
+    def back_z_copy(s, h):
+        return remote(
+            tok_z.at[s, :, columns(h)], back_z.at[s, :, columns(h)],
+            bz_send.at[s, h], bz_recv.at[s, h], "expert", z_peer(s),
+        )
+
+    def back_near_copy(s, h):
+        return remote(
+            tok_z.at[s, :, columns(h)], back_z.at[s, :, columns(h)],
+            bz_send.at[s, h], bz_recv.at[s, h], "expert", z_peer(1),
+        )
 
     def each(first, last, body):
         def step(i, carry):
@@ -159,15 +162,17 @@
     direct = [(2, 0), (1, 1), (2, 1), (1, 0)] if relayed else [(k, h) for k in range(1, nt) for h in range(2)]
     peers = sorted({k for k, _ in direct})
 
+    own_steps = [s for s in range(1, ne) if s == 1 or s % 2 == 0]
+
     tok_load.wait()
     pl.semaphore_wait(barrier, ne - 1 + nt - 1)
     for k, h in direct:
         tok_t_copy(k, h).start()
-    for s in range(2, ne, 2):
+    for s in own_steps:
         tok_z_copy(s).start()
     for k in range(1, nt):
         meta_t_copy(k).start()
-    for s in range(2, ne):
+    for s in range(1, ne):
         meta_z_copy(s).start()
     for load in loads:
         load.start()
@@ -180,13 +185,6 @@
 
     def weigher(place_row, weight_row):
         return jnp.where(slots == place_row, weight_row, 0.0).astype(BF)
-
-    def near(k):
-        pick = picker(meta_t[k, z_peer(1), pl.ds(t, 1), :])
-        for c, w in pieces(width, 512):
-            stage[1, k * cap:(k + 1) * cap, c:c + w] = jnp.dot(
-                pick, tok_t[k, :, c:c + w], preferred_element_type=F32).astype(BF)
-        near_copy(k).start()
 
     def dispatch(s):
         for k in [*range(1, nt), 0]:
@@ -223,7 +221,6 @@
         for c, w in pieces(width, 256):
             rows[s, :, c:c + w] = jnp.dot(hidden[...], wd[:, c:c + w], preferred_element_type=F32).astype(BF)
 
-    near(0)
     if relayed:
         tok_t_copy(2, 0).wait_recv()
         relay_copy(0).start()
@@ -232,17 +229,16 @@
         rest = [(2, 1), (1, 0)]
     else:
         rest = direct
+    tok_z_copy(1).wait_recv()
+    meta_z_copy(1).wait_recv()
+    dispatch(1)
     for k, h in rest:
         tok_t_copy(k, h).wait_recv()
     for k in range(1, nt):
         meta_t_copy(k).wait_recv()
-    for k in peers:
-        near(k)
-    each(1, ne // 2, dispatch_even)
     if relayed:
         for h in range(2):
             relay_copy(h).wait_recv()
-        near(3)
 
     for load in loads[:3]:
         load.wait()
@@ -254,7 +250,7 @@
         u = lax.dot_general(x, su[c:c + w, :], nk, preferred_element_type=F32)
         hidden_s[:, c:c + w] = (g / (1.0 + jnp.exp(-g)) * u).astype(BF)
 
-    each(1, ne // 2, dispatch_odd)
+    each(1, ne // 2, dispatch_even)
 
     for c, w in pieces(width, 256):
         part_s[:, c:c + w] = jnp.dot(hidden_s[...], sd[:, c:c + w], preferred_element_type=F32).astype(BF)
@@ -267,35 +263,31 @@
             rows[0, k * cap:(k + 1) * cap, c:c + w] = jnp.dot(
                 pick, tok_t[k, :, c:c + w], preferred_element_type=F32).astype(BF)
 
+    for k in range(1, nt):
+        dispatch_copy(1, k).wait_recv()
+    expert(1)
+    near_back_copy().start()
+    each(1, ne // 2, dispatch_odd)
+
     def routed_stage(i):
-        pairs = ne // 2
-        s = jnp.where(i < pairs - 1, 2 * i + 2, 2 * (i - pairs) + 3)
-        s = jnp.where(i == pairs - 1, 1, s)
-        s = jnp.where(i == ne - 1, 0, s)
-
-        @pl.when(s == 1)
-        def _():
-            for k in range(nt):
-                near_copy(k).wait_recv()
-
-        @pl.when(s > 1)
+        evens = ne // 2 - 1
+        s = jnp.where(i < evens, 2 * i + 2, 2 * (i - evens) + 3)
+        s = jnp.where(i == ne - 2, 0, s)
+
+        @pl.when(s > 0)
         def _():
             for k in range(1, nt):
                 dispatch_copy(s, k).wait_recv()
 
         expert(s)
 
-        @pl.when(s == 1)
-        def _():
-            near_back_copy().start()
-
-        @pl.when(s > 1)
+        @pl.when(s > 0)
         def _():
             for k in range(1, nt):
                 return_copy(s, k).start()
             back[s, 0:cap] = rows[s, 0:cap]
 
-    each(0, ne, routed_stage)
+    each(0, ne - 1, routed_stage)
 
     flip = (((0,), (0,)), ((), ()))
 
@@ -310,22 +302,24 @@
     def combine_odd(j):
         s = 2 * j + 1
         parts = combined(s)
-        for c, w in pieces(width, 512):
-            tok_z[s, :, c:c + w] = lax.dot_general(
-                parts, back[s, :, c:c + w], flip, preferred_element_type=F32).astype(BF)
-        back_near_copy(s).start()
+        for h in range(2):
+            for c, w in pieces(width // 2, 512):
+                c = c + h * (width // 2)
+                tok_z[s, :, c:c + w] = lax.dot_general(
+                    parts, back[s, :, c:c + w], flip, preferred_element_type=F32).astype(BF)
+            back_near_copy(s, h).start()
 
     def combine_even(j):
         s = 2 * j
         parts = combined(s)
         forward_copy(s + 1).wait_send()
-        back_near_copy(s + 1).wait_recv()
-        for c, w in pieces(width, 512):
-            got = lax.dot_general(parts, back[s, :, c:c + w], flip, preferred_element_type=F32)
-            tok_z[s, :, c:c + w] = (got + back_z[s + 1, :, c:c + w].astype(F32)).astype(BF)
-        back_z_copy(s).start()
-
-    each(1, ne // 2, combine_odd)
+        for h in range(2):
+            back_near_copy(s + 1, h).wait_recv()
+            for c, w in pieces(width // 2, 512):
+                c = c + h * (width // 2)
+                got = lax.dot_general(parts, back[s, :, c:c + w], flip, preferred_element_type=F32)
+                tok_z[s, :, c:c + w] = (got + back_z[s + 1, :, c:c + w].astype(F32)).astype(BF)
+            back_z_copy(s, h).start()
 
     for k, h in direct:
         tok_t_copy(k, h).wait_send()
@@ -351,7 +345,7 @@
                 now = slice((1 - k % 2) * half, (2 - k % 2) * half)
                 later = slice((k % 2) * half, (k % 2 + 1) * half)
                 tok_t[k, now, c:c + w] = got[now].astype(BF)
-                held[k, :, c:c + w] = got[later]
+                held[k - 1, :, c:c + w] = got[later]
             else:
                 tok_t[k, :, c:c + w] = got.astype(BF)
         if relayed and k == 3:
@@ -362,11 +356,12 @@
         elif k:
             for h in range(2):
                 back_t_copy(k, h).start()
+    each(1, ne // 2, combine_odd)
     if relayed:
         for k in (1, 2):
             h = k % 2
             back_relay_copy(h).wait_recv()
-            tok_t[k, part_rows(h), :] = (held[k] + back_t[3, part_rows(h), :].astype(F32)).astype(BF)
+            tok_t[k, part_rows(h), :] = (held[k - 1] + back_t[3, part_rows(h), :].astype(F32)).astype(BF)
             back_t_copy(k, h).start()
 
     each(1, ne // 2, combine_even)
@@ -376,22 +371,24 @@
             back_t_copy(k, h).wait_recv()
         total[...] += back_t[k].astype(F32)
     for s in range(2, ne, 2):
-        back_z_copy(s).wait_recv()
+        for h in range(2):
+            back_z_copy(s, h).wait_recv()
         total[...] += back_z[s].astype(F32)
     out_ref[...] = total[...].astype(BF)
 
-    for k in range(nt):
-        near_copy(k).wait_send()
     near_back_copy().wait_send()
-    for s in range(2, ne):
+    for s in range(1, ne):
         meta_z_copy(s).wait_send()
         for k in range(1, nt):
             dispatch_copy(s, k).wait_send()
-            return_copy(s, k).wait_send()
+            if s > 1:
+                return_copy(s, k).wait_send()
+    for s in own_steps:
+        tok_z_copy(s).wait_send()
     for s in range(2, ne, 2):
-        tok_z_copy(s).wait_send()
-        back_z_copy(s).wait_send()
-        back_near_copy(s + 1).wait_send()
+        for h in range(2):
+            back_z_copy(s, h).wait_send()
+            back_near_copy(s + 1, h).wait_send()
     for k in range(1, nt):
         meta_t_copy(k).wait_send()
     for k, h in direct:
@@ -442,12 +439,12 @@
             pltpu.VMEM((nt * tok, inner_s), BF),
             pltpu.VMEM((nt * tok, width), BF),
             pltpu.VMEM((tok, width), F32),
-            pltpu.VMEM((3, tok // 2, width), F32),
+            pltpu.VMEM((2, tok // 2, width), F32),
             dma((7,)),
             dma((ne,)), dma((ne,)), dma((nt,)), dma((nt,)),
             dma((ne,)), dma((ne,)), dma((nt, 2)), dma((nt, 2)),
             dma((ne, nt)), dma((ne, nt)), dma((ne, nt)), dma((ne, nt)),
-            dma((nt, 2)), dma((nt, 2)), dma((ne,)), dma((ne,)),
+            dma((nt, 2)), dma((nt, 2)), dma((ne, 2)), dma((ne, 2)),
         ],
         compiler_params=pltpu.CompilerParams(
             collective_id=0, has_side_effects=True, vmem_limit_bytes=67043328

time: 130 us -> 124 us (0.954)
  Pallas kernels: 126 us -> 120 us
    pallas_call x1, Pallas kernels: 126 us -> 120 us  [per_device(): pl.pallas_call(functools.partial(layer_kernel, ne, nt, cap), out_shape=ja...]
where the time goes in v3:
time: 124 us; the launch traced here: 123 us
  Pallas kernels  120 us (97%)
  local copies, waits for them, and re-layouts  3.17 us (3%)
    pallas_call x1, Pallas kernels, per_device(): pl.pallas_call(functools.partial(layer_kernel, ne, nt, cap), out_shape=ja...  120 us

profile of v3, /device:TPU:0, one launch (start us, length us, event | category | flops | bytes accessed | tf_op | source)
XLA Modules:
  0.0 123.0 jit_solution(2194189017943174816)
XLA Ops:
  0.0 1.3 %reshape.3.gate_ref = bf16[1,2048]{1,0:T(2,128)(2,1)} reshape(bf16[2048]{0:T(1024)(128)(2,1)} %param.19) | data formatting | bytes 8192 | tf_op jit(solution)/shard_map/reshape | solution.py:455
  1.3 119.8 %moe_layer.1 = bf16[128,2048]{1,0:T(8,128)(2,1)} custom-call(bf16[128,2048]{1,0:T(8,128)(2,1)} %tok_hbm.1, s32[4,128]{1,0:T(4,128)} %bitcast.6, f32[4,128]{1,0:T(4,128)} %bitcast.7, bf16[1,2048,1408]{2,1,0:T(8,128)(2,1)} %wg_hbm.1, bf16[1,2048,1408]{2,1,0:T(8,128)(2,1)} %wu_hbm.1, bf16[1,1408,2048]{2,1,0:T(8,128)(2,1)} %wd_hbm.1, bf16[704,2048]{1,0:T(8,128)(2,1)} %bitcast.4, ...), custom_call_target="tpu_custom_call" | custom-call | tf_op jit(solution)/shard_map/moe_layer/pallas_call | solution.py:416
  121.1 1.9 %copy.12 = bf16[128,2048]{1,0:T(8,128)(2,1)} copy(bf16[128,2048]{1,0:T(8,128)(2,1)} %moe_layer.1) | data formatting | bytes 1048576
